TPU v7x, 32 devices: a whole 2x2x4 slice. The times are simulated.
32 devices in a mesh: groups: 2 (over y), ctx: 4 (over z), fsdp: 2 (over x), dp: 2 (over core).
Axes of the slice: x: 2, y: 2, z: 4, core: 2. Of those that a mesh axis runs over, the one named last changes fastest.
Arguments:
- query_in: bfloat16 [8, 512, 1024], P(('groups', 'fsdp', 'dp'), 'ctx'), parts along dimension 0, may hold values from -11 to 11
- key_in: bfloat16 [8, 512, 1024], P(('groups', 'fsdp', 'dp'), 'ctx'), parts along dimension 0, may hold values from -11 to 11
- value_in: bfloat16 [8, 512, 1024], P(('groups', 'fsdp', 'dp'), 'ctx'), parts along dimension 0, may hold values from -6 to 6
- utt_lengths: int32 [8], P(('groups', 'fsdp', 'dp')), parts along dimension 0, may hold values from 128 to 512, as said below
- frames_in: bfloat16 [8, 512, 1536], P(('groups', 'fsdp', 'dp'), 'ctx'), parts along dimension 0, may hold values from -6 to 6
- out_weight: bfloat16 [1024, 1536], P(None, 'fsdp'), may hold values from -1.5 to 1.5
- conv_kernel: float32 [31, 1536], P(None, 'fsdp'), may hold values from -1 to 1
- conv_bias: float32 [1536], P('fsdp'), may hold values from -3 to 3
- ln_gain: float32 [1536], P('fsdp'), may hold values from 0.1 to 1.9
- cotangent: bfloat16 [8, 512, 1536], P(('groups', 'fsdp', 'dp'), 'ctx'), parts along dimension 0, may hold values from -6 to 6
Outputs:
- block_out: bfloat16 [8, 512, 1536], P(('groups', 'fsdp', 'dp'), 'ctx'), parts along dimension 0
- hidden_grad: bfloat16 [8, 512, 1536], P(('groups', 'fsdp', 'dp'), 'ctx'), parts along dimension 0
- grad_kernel: float32 [62, 1536], P('groups', 'fsdp'), parts along dimension 0
- grad_bias: float32 [3072], P(('groups', 'fsdp')), parts along dimension 0
- grad_gain: float32 [3072], P(('groups', 'fsdp')), parts along dimension 0
There are 2 independent parts, one for each index of `groups`. A program takes and returns all parts, laid end to end along the dimension named above; an argument that names none is the same for every part. Nothing has to cross between parts.
Inputs may be any that keep to these rules, and one draw needn't show every extreme that they name: `utt_lengths`: in every group one utterance is full, of 512 valid frames.
All inputs are finite; a program needn't handle non-finite values.
Results may differ from a plain program's by a relative error of at most 0.019.
Values may be sent and summed in bfloat16 or wider, within the bound.
No kernel may reach another device: no remote copies, remote signals or barrier semaphores. Data moves between devices by JAX's collectives and lax.ppermute only.
A program may use at most 64 MiB of HBM per device.

v0:
```python
import math
import jax
import jax.numpy as jnp
from jax import lax
from jax.sharding import PartitionSpec as P

HD = 64
TAPS = 31
NEG_FILL = -1e30


def extended(block, sides, width):
    for axis, dim in sides:
        count = lax.axis_size(axis)
        forward = [(i, i + 1) for i in range(count - 1)]
        backward = [(target, source) for source, target in forward]
        low = lax.ppermute(
            lax.slice_in_dim(block, block.shape[dim] - width, None, axis=dim), axis, forward
        )
        high = lax.ppermute(lax.slice_in_dim(block, 0, width, axis=dim), axis, backward)
        block = jnp.concatenate([low, block, high], axis=dim)
    return block


def absorb_block(state, query_heads, key_heads, value_heads, key_start, valid_len):
    run_max, run_sum, summed = state
    scores = jnp.einsum(
        "qhd,khd->qhk", query_heads, key_heads, preferred_element_type=jnp.float32
    ) * (1.0 / math.sqrt(HD))
    usable = key_start + jnp.arange(key_heads.shape[0]) < valid_len
    scores = jnp.where(usable, scores, NEG_FILL)
    new_max = jnp.maximum(run_max, jnp.max(scores, axis=-1))
    rescale = jnp.exp(run_max - new_max)
    weights = jnp.where(usable, jnp.exp(scores - new_max[..., None]), 0.0)
    run_sum = run_sum * rescale + jnp.sum(weights, axis=-1)
    summed = summed * rescale[..., None] + jnp.einsum(
        "qhk,khd->qhd",
        weights.astype(jnp.bfloat16),
        value_heads,
        preferred_element_type=jnp.float32,
    )
    return (new_max, run_sum, summed)


def normalize(block):
    as_float = block.astype(jnp.float32)
    average = jnp.mean(as_float, axis=-1, keepdims=True)
    centered = as_float - average
    variance = jnp.mean(centered * centered, axis=-1, keepdims=True)
    inv_scale = lax.rsqrt(variance + 1e-05)
    return (centered * inv_scale, inv_scale)


def convolve(conv_in, kernel_all, bias_all, out_rows):
    pre_act = bias_all + jnp.zeros((out_rows, conv_in.shape[1]), jnp.float32)
    for tap_index in range(TAPS):
        pre_act = pre_act + kernel_all[tap_index] * conv_in[tap_index : tap_index + out_rows]
    return pre_act


def live_of(positions, valid_len):
    return ((positions >= 0) & (positions < valid_len)).astype(jnp.float32)[:, None]


def shards(
    query_in,
    key_in,
    value_in,
    utt_lengths,
    frames_in,
    out_weight,
    conv_kernel,
    conv_bias,
    ln_gain,
    cotangent,
):
    row_count = query_in.shape[1]
    feat_width = query_in.shape[2]
    head_count = feat_width // HD
    valid_len = utt_lengths[0]
    ctx_count = lax.axis_size("ctx")
    row_offset = lax.axis_index("ctx") * row_count
    half_taps = TAPS // 2
    query_heads = query_in[0].reshape(row_count, head_count, HD)
    start_state = (
        jnp.full((row_count, head_count), NEG_FILL, jnp.float32),
        jnp.zeros((row_count, head_count), jnp.float32),
        jnp.zeros((row_count, head_count, HD), jnp.float32),
    )
    state = start_state
    first_row = jnp.int32(0)
    key_part = lax.all_gather(key_in, "ctx", axis=1, tiled=True)
    value_part = lax.all_gather(value_in, "ctx", axis=1, tiled=True)
    piece_rows = key_part.shape[1]
    block_len = math.gcd(piece_rows, 512)
    for block_start in range(0, piece_rows, block_len):
        key_heads = key_part[0, block_start : block_start + block_len].reshape(
            block_len, head_count, HD
        )
        value_heads = value_part[0, block_start : block_start + block_len].reshape(
            block_len, head_count, HD
        )
        state = absorb_block(
            state, query_heads, key_heads, value_heads, first_row + block_start, valid_len
        )
    run_max, run_sum, summed = state
    attended = (summed / run_sum[..., None]).reshape(row_count, feat_width).astype(jnp.bfloat16)
    projected = jnp.dot(
        attended,
        lax.all_gather(out_weight, "fsdp", axis=1, tiled=True),
        preferred_element_type=jnp.float32,
    )
    hidden = (frames_in[0].astype(jnp.float32) + projected).astype(jnp.bfloat16)
    kernel_all, bias_all, gain_all = (
        lax.all_gather(conv_kernel, "fsdp", axis=1, tiled=True),
        lax.all_gather(conv_bias, "fsdp", axis=0, tiled=True),
        lax.all_gather(ln_gain, "fsdp", axis=0, tiled=True),
    )
    grad_in = cotangent[0].astype(jnp.float32)
    live_mask = live_of(row_offset + jnp.arange(row_count), valid_len)
    widened = extended(hidden, (("ctx", 0),), half_taps)
    normed_ext, inv_ext = normalize(widened)
    conv_in = (
        live_of(row_offset - half_taps + jnp.arange(row_count + 2 * half_taps), valid_len)
        * normed_ext
        * gain_all
    )
    pre_act = convolve(conv_in, kernel_all, bias_all, row_count)
    gate_val = jax.nn.sigmoid(pre_act)
    grad_pre = grad_in * live_mask * gate_val * (1.0 + pre_act * (1.0 - gate_val))
    grad_wide = extended(grad_pre.astype(jnp.bfloat16), (("ctx", 0),), half_taps).astype(
        grad_pre.dtype
    )
    normed = normed_ext[half_taps : half_taps + row_count]
    inv_scale = inv_ext[half_taps : half_taps + row_count]
    block_out = (hidden.astype(jnp.float32) + live_mask * pre_act * gate_val).astype(jnp.bfloat16)
    grad_conv = jnp.zeros((row_count, grad_pre.shape[1]), jnp.float32)
    kernel_rows = []
    for tap_index in range(TAPS):
        back = 2 * half_taps - tap_index
        grad_conv = grad_conv + kernel_all[tap_index] * grad_wide[back : back + row_count]
        kernel_rows.append(jnp.sum(grad_pre * conv_in[tap_index : tap_index + row_count], axis=0))
    grad_conv = live_mask * grad_conv
    grad_hat = grad_conv * gain_all
    first_mean = jnp.mean(grad_hat, axis=-1, keepdims=True)
    second_mean = jnp.mean(grad_hat * normed, axis=-1, keepdims=True)
    hidden_grad = (grad_in + (grad_hat - first_mean - normed * second_mean) * inv_scale).astype(
        jnp.bfloat16
    )
    factor = 1.0 / math.sqrt(lax.axis_size("fsdp") * lax.axis_size("dp") * row_count * ctx_count)
    kernel_term = jnp.stack(kernel_rows) * factor
    bias_term = (jnp.sum(grad_pre, axis=0) * factor)[None]
    gain_term = (jnp.sum(grad_conv * normed, axis=0) * factor)[None]
    shares = (
        lax.psum_scatter(
            kernel_term.astype(jnp.bfloat16), "fsdp", scatter_dimension=1, tiled=True
        ).astype(jnp.float32),
        lax.psum_scatter(
            bias_term.astype(jnp.bfloat16), "fsdp", scatter_dimension=1, tiled=True
        ).astype(jnp.float32),
        lax.psum_scatter(
            gain_term.astype(jnp.bfloat16), "fsdp", scatter_dimension=1, tiled=True
        ).astype(jnp.float32),
    )
    totals = lax.psum((shares[0], shares[1], shares[2]), ("ctx", "dp"))
    return (block_out[None], hidden_grad[None], totals[0], totals[1][0], totals[2][0])


def solution(mesh):
    in_specs = (
        P(("groups", "fsdp", "dp"), "ctx", None),
        P(("groups", "fsdp", "dp"), "ctx", None),
        P(("groups", "fsdp", "dp"), "ctx", None),
        P(("groups", "fsdp", "dp")),
        P(("groups", "fsdp", "dp"), "ctx", None),
        P(None, "fsdp"),
        P(None, "fsdp"),
        P("fsdp"),
        P("fsdp"),
        P(("groups", "fsdp", "dp"), "ctx", None),
    )
    out_specs = (
        P(("groups", "fsdp", "dp"), "ctx", None),
        P(("groups", "fsdp", "dp"), "ctx", None),
        P("groups", "fsdp"),
        P(("groups", "fsdp")),
        P(("groups", "fsdp")),
    )
    return jax.shard_map(shards, mesh=mesh, in_specs=in_specs, out_specs=out_specs, check_vma=False)
```

profile of v0, /device:TPU:0, one launch (start us, length us, event | category | flops | bytes accessed | tf_op | source)
XLA Modules:
  0.0 231.5 jit_solution(14485959095688557060)
XLA Ops:
  10.1 1.1 copy.24
  11.2 6.7 %all_gather.22 = f32[31,1536]{1,0:T(8,128)S(1)} all-gather(f32[31,768]{1,0:T(8,128)} %param.16), channel_id=1, replica_groups=mesh['groups'=2,'ctx'=4,'fsdp'=2,'dp'=2] {'fsdp'}, dimensions={1}, use_global_device_ids=true | all-gather | bytes 285696 | tf_op jit(solution)/shard_map/all_gather | solution.py:115
  18.4 21.8 %all-gather.6.cloned.1.call-done = bf16[1,512,1024]{2,1,0:T(8,128)(2,1)} async-done(((bf16[1,128,1024]{2,1,0:T(8,128)(2,1)}), bf16[1,512,1024]{2,1,0:T(8,128)(2,1)}) %all-gather.6.cloned.1.call-update) | async-done | bytes 1048592 | tf_op jit(solution)/shard_map/all_gather | solution.py:92
  40.2 1.5 copy.23
  41.7 27.5 %all-gather.8.cloned.1.call-done = bf16[1,512,1024]{2,1,0:T(8,128)(2,1)} async-done(((bf16[1,128,1024]{2,1,0:T(8,128)(2,1)}), bf16[1,512,1024]{2,1,0:T(8,128)(2,1)}) %all-gather.8.cloned.1.call-update) | async-done | bytes 1048592 | tf_op jit(solution)/shard_map/all_gather | solution.py:93
  69.3 1.5 copy.25
  70.8 1.1 bitcast_reduce_fusion
  71.9 1.2 fusion.2
  73.1 1.5 fusion.20
  74.6 40.7 %all-gather.10.cloned.1.call-done = bf16[1024,1536]{1,0:T(8,128)(2,1)} async-done(((bf16[1024,768]{1,0:T(8,128)(2,1)}), bf16[1024,1536]{1,0:T(8,128)(2,1)}) %all-gather.10.cloned.1.call-update) | async-done | bytes 3145744 | tf_op jit(solution)/shard_map/all_gather | solution.py:110
  115.3 2.5 %fusion.4 = bf16[128,1536]{1,0:T(8,128)(2,1)S(1)} fusion(bf16[128,1024]{0,1:T(8,128)(2,1)S(1)} %bitcast.62, bf16[1024,1536]{1,0:T(8,128)(2,1)} %all-gather.10.cloned.1.call-done, bf16[1,128,1536]{2,1,0:T(8,128)(2,1)S(1)} %copy-done.1), kind=kOutput, calls=%fused_computation.8 | convolution fusion | flops 403243008 | bytes 4194304 | tf_op jit(solution)/shard_map/dot_general | solution.py:108
  117.8 3.4 %collective-permute-start = (bf16[15,1536]{1,0:T(8,128)(2,1)S(1)}, bf16[15,1536]{1,0:T(8,128)(2,1)S(1)}, u32[]{:S(2)}, u32[]{:S(2)}) collective-permute-start(bf16[15,1536]{1,0:T(8,128)(2,1)S(1)} %get-tuple-element.82), channel_id=1, source_target_pairs={{0,4},{4,8},{8,12},{1,5},{5,9},{9,13},{2,6},{6,10},{10,14},{3,7},{... | collective-permute-start | bytes 138248 | tf_op jit(solution)/shard_map/ppermute | solution.py:17
  121.2 1.3 collective-permute-start.1
  122.5 4.3 %all-gather.1 = f32[2,1,768]{2,1,0:T(1,128)S(1)} all-gather(f32[1,1,768]{2,1,0:T(1,128)S(1)} %reshape.114), channel_id=1, replica_groups=mesh['groups'=2,'ctx'=4,'fsdp'=2,'dp'=2] {'fsdp'}, dimensions={0}, use_global_device_ids=true | all-gather | bytes 9216 | tf_op jit(solution)/shard_map/all_gather | solution.py:117
  126.9 4.3 %all-gather = f32[2,1,768]{2,1,0:T(1,128)S(1)} all-gather(f32[1,1,768]{2,1,0:T(1,128)S(1)} %reshape.112), channel_id=1, replica_groups=mesh['groups'=2,'ctx'=4,'fsdp'=2,'dp'=2] {'fsdp'}, dimensions={0}, use_global_device_ids=true | all-gather | bytes 9216 | tf_op jit(solution)/shard_map/all_gather | solution.py:116
  132.3 6.3 %multiply_reduce_fusion.1 = (f32[1536]{0:T(1024)S(1)}, f32[1536]{0:T(1024)S(1)}, f32[1536]{0:T(1024)S(1)}, f32[1536]{0:T(1024)S(1)}, f32[1536]{0:T(1024)S(1)}, /...) fusion(f32[158,1536]{1,0:T(8,128)S(1)} %get-tuple-element.79, ...), kind=kLoop, calls=%fused_computation.90 | loop fusion | flops 21206016 | bytes 26653184 | tf_op jit(solution)/shard_map/reduce_sum | solution.py:142
  138.6 2.1 multiply_reduce_fusion.19
  140.8 4.5 %collective-permute-start.2 = (bf16[15,1536]{1,0:T(8,128)(2,1)S(1)}, bf16[15,1536]{1,0:T(8,128)(2,1)S(1)}, u32[]{:S(2)}, u32[]{:S(2)}) collective-permute-start(bf16[15,1536]{1,0:T(8,128)(2,1)S(1)} %get-tuple-element.80), channel_id=1, source_target_pairs={{0,4},{4,8},{8,12},{1,5},{5,9},{9,13},{2,6},{6,10},{10,14},{3,7},{... | collective-permute-start | bytes 138248 | tf_op jit(solution)/shard_map/ppermute | solution.py:17
  145.3 1.3 collective-permute-start.3
  147.9 1.7 fusion.59
  159.4 6.1 %multiply_reduce_fusion = (f32[1536]{0:T(1024)S(1)}, f32[128]{0:T(128)S(1)}, f32[128]{0:T(128)S(1)}, f32[128,1536]{1,0:T(8,128)S(1)}) fusion(f32[158,1536]{1,0:T(8,128)S(1)} %get-tuple-element.78, f32[1536]{0:T(1024)S(1)} %reshape.115, f32[158,1536]{1,0:T(8,128)S(1)} %maximum_convert_fusion, f32[1536]{0:T(1024)S(1)} %get-tuple-element.41, ...), kind=kLoop, calls=%fused_computation.89 | loop fusion | flops 13367552 | bytes 26156544 | tf_op jit(solution)/shard_map/reduce_sum | solution.py:153
  169.5 11.5 %reduce-scatter.12.cloned.1.call-done = bf16[768,1]{1,0:T(8,128)(2,1)} async-done(((bf16[1536,1]{1,0:T(8,128)(2,1)}), bf16[768,1]{1,0:T(8,128)(2,1)}) %reduce-scatter.12.cloned.1.call-update) | async-done | bytes 1552
  182.1 11.6 %reduce-scatter.8.cloned.1.call-done = bf16[31,768]{1,0:T(8,128)(2,1)} async-done(((bf16[31,1536]{1,0:T(8,128)(2,1)}), bf16[31,768]{1,0:T(8,128)(2,1)}) %reduce-scatter.8.cloned.1.call-update) | async-done | bytes 47632 | tf_op jit(solution)/shard_map/reduce_scatter | solution.py:155
  193.7 31.0 %all-reduce.2 = (f32[31,768]{1,0:T(8,128)}, f32[768]{0:T(1024)}, f32[768]{0:T(1024)}) all-reduce(bf16[31,768]{1,0:T(8,128)(2,1)} %reduce-scatter.8.cloned.1.call-done, f32[768]{0:T(1024)S(1)} %get-tuple-element.91, f32[768]{0:T(1024)S(1)} %get-tuple-element.90), channel_id=1, replica_groups=mesh['groups'=2,'ctx'=4,'fsdp'=2,'dp'=2] {'ctx','dp'}, use_global_device_ids=true, to_apply=%region_38.39 | all-reduce | flops 25344 | bytes 155136 | tf_op jit(solution)/shard_map/psum | solution.py:165
  (95 shorter events, 19.8 us)
Async XLA Ops:
  7.2 33.1 %all-gather.6.cloned.1.call-start = ((), (), s32[]{:S(2)}) async-start(), calls=%async_computation.3 | async-start | bytes 1310720 | tf_op jit(solution)/shard_map/all_gather | solution.py:92
  7.9 61.4 %all-gather.8.cloned.1.call-start = ((), (), s32[]{:S(2)}) async-start(), calls=%async_computation.4 | async-start | bytes 1310720 | tf_op jit(solution)/shard_map/all_gather | solution.py:93
  8.6 106.6 %all-gather.10.cloned.1.call-start = ((), (), s32[]{:S(2)}) async-start(), calls=%async_computation.5 | async-start | bytes 4718592 | tf_op jit(solution)/shard_map/all_gather | solution.py:110
  9.4 158.0 %reduce-scatter.10.cloned.1.call-start = ((), (), s32[]{:S(2)}) async-start(), calls=%async_computation.7 | async-start | bytes 589824
  73.1 42.2 %copy-start.1 = (bf16[1,128,1536]{2,1,0:T(8,128)(2,1)S(1)}, bf16[1,128,1536]{2,1,0:T(8,128)(2,1)}, u32[]{:S(2)}) copy-start(bf16[1,128,1536]{2,1,0:T(8,128)(2,1)} %param.14) | copy-start | bytes 1179652
  74.5 48.0 %copy-start.5 = (f32[768]{0:T(1024)S(1)}, f32[768]{0:T(1024)}, u32[]{:S(2)}) copy-start(f32[768]{0:T(1024)} %param.18) | copy-start | bytes 9220
  74.5 52.4 %copy-start.6 = (f32[768]{0:T(1024)S(1)}, f32[768]{0:T(1024)}, u32[]{:S(2)}) copy-start(f32[768]{0:T(1024)} %param.17) | copy-start | bytes 9220
  74.6 57.7 %copy-start = (bf16[1,128,1536]{2,1,0:T(8,128)(2,1)S(1)}, bf16[1,128,1536]{2,1,0:T(8,128)(2,1)}, u32[]{:S(2)}) copy-start(bf16[1,128,1536]{2,1,0:T(8,128)(2,1)} %param.19) | copy-start | bytes 1179652
  117.8 13.5 %collective-permute-start = (bf16[15,1536]{1,0:T(8,128)(2,1)S(1)}, bf16[15,1536]{1,0:T(8,128)(2,1)S(1)}, u32[]{:S(2)}, u32[]{:S(2)}) collective-permute-start(bf16[15,1536]{1,0:T(8,128)(2,1)S(1)} %get-tuple-element.82), channel_id=1, source_target_pairs={{0,4},{4,8},{8,12},{1,5},{5,9},{9,13},{2,6},{6,10},{10,14},{3,7},{... | collective-permute-start | bytes 138248 | tf_op jit(solution)/shard_map/ppermute | solution.py:17
  121.2 10.1 %collective-permute-start.1 = (bf16[15,1536]{1,0:T(8,128)(2,1)S(1)}, bf16[15,1536]{1,0:T(8,128)(2,1)S(1)}, u32[]{:S(2)}, u32[]{:S(2)}) collective-permute-start(bf16[15,1536]{1,0:T(8,128)(2,1)S(1)} %get-tuple-element.83), channel_id=1, source_target_pairs={{4,0},{8,4},{12,8},{5,1},{9,5},{13,9},{6,2},{10,6},{14,10},{7,3},{... | collective-permute-start | bytes 138248 | tf_op jit(solution)/shard_map/ppermute | solution.py:20
  122.5 16.1 %copy-start.2 = (f32[128]{0:T(128)}, f32[128]{0:T(128)S(1)}, u32[]{:S(2)}) copy-start(f32[128]{0:T(128)S(1)} %and_convert_fusion.1) | copy-start | bytes 1540
  131.9 6.7 %copy-start.3 = (f32[158]{0:T(256)}, f32[158]{0:T(256)S(1)}, u32[]{:S(2)}) copy-start(f32[158]{0:T(256)S(1)} %add_rsqrt_fusion) | copy-start | bytes 1900
  140.8 18.5 %collective-permute-start.2 = (bf16[15,1536]{1,0:T(8,128)(2,1)S(1)}, bf16[15,1536]{1,0:T(8,128)(2,1)S(1)}, u32[]{:S(2)}, u32[]{:S(2)}) collective-permute-start(bf16[15,1536]{1,0:T(8,128)(2,1)S(1)} %get-tuple-element.80), channel_id=1, source_target_pairs={{0,4},{4,8},{8,12},{1,5},{5,9},{9,13},{2,6},{6,10},{10,14},{3,7},{... | collective-permute-start | bytes 138248 | tf_op jit(solution)/shard_map/ppermute | solution.py:17
  145.3 14.0 %collective-permute-start.3 = (bf16[15,1536]{1,0:T(8,128)(2,1)S(1)}, bf16[15,1536]{1,0:T(8,128)(2,1)S(1)}, u32[]{:S(2)}, u32[]{:S(2)}) collective-permute-start(bf16[15,1536]{1,0:T(8,128)(2,1)S(1)} %get-tuple-element.81), channel_id=1, source_target_pairs={{4,0},{8,4},{12,8},{5,1},{9,5},{13,9},{6,2},{10,6},{14,10},{7,3},{... | collective-permute-start | bytes 138248 | tf_op jit(solution)/shard_map/ppermute | solution.py:20
  147.7 33.4 %reduce-scatter.12.cloned.1.call-start = ((), (), s32[]{:S(2)}) async-start(), calls=%async_computation.8 | async-start | bytes 589824
  159.4 7.9 %copy-start.4 = (f32[158]{0:T(256)S(1)}, f32[158]{0:T(256)}, u32[]{:S(2)}) copy-start(f32[158]{0:T(256)} %copy-done.3) | copy-start | bytes 1900
  166.6 27.1 %reduce-scatter.8.cloned.1.call-start = ((), (), s32[]{:S(2)}) async-start(), calls=%async_computation.6 | async-start | bytes 147456 | tf_op jit(solution)/shard_map/reduce_scatter | solution.py:155
Sparse Core Ops, SparseCore 0:
  9.6 30.6 all-gather.5
  41.8 27.4 all-gather.7
  70.8 44.4 all-gather.9
  147.8 14.2 reduce-scatter.9
  166.7 14.2 reduce-scatter.11
  183.6 9.9 reduce-scatter.7
where the time goes:
time: 233 us; the launch traced here: 232 us
  waiting for transfers between devices  115 us (49%)
  blocking collectives  46.4 us (20%)
  other arithmetic  20.3 us (9%)
  local copies, waits for them, and re-layouts  18.4 us (8%)
  between operations  15.2 us (7%)
  starting transfers between devices  10.9 us (5%)
  matrix products  5.07 us (2%)
    all_gather x1, waiting for transfers between devices, shards(): lax.all_gather(out_weight, 'fsdp', axis=1, tiled=True)  40.7 us
    psum x1, blocking collectives, shards(): totals = lax.psum((shares[0], shares[1], shares[2]), ('ctx', 'dp'))  31 us
    all_gather x1, waiting for transfers between devices, shards(): value_part = lax.all_gather(value_in, 'ctx', axis=1, tiled=True)  27.5 us
    all_gather x1, waiting for transfers between devices, shards(): key_part = lax.all_gather(key_in, 'ctx', axis=1, tiled=True)  21.8 us
    unnamed x8, waiting for transfers between devices  13.6 us
    reduce_scatter x1, waiting for transfers between devices, shards(): lax.psum_scatter(kernel_term.astype(jnp.bfloat16), 'fsdp', scatter_dimens...  11.6 us
    another operation x32, local copies, waits for them, and re-layouts, shards(): kernel_term = jnp.stack(kernel_rows) * factor  9.55 us
    reduce_sum x2, other arithmetic, shards(): jnp.sum(grad_pre * conv_in[tap_index:tap_index + row_count], axis=0)  8.42 us
  transfers between devices with their start and end apart: 10, of which 5 were waited for; matrix products, arithmetic and copies ran while one was open for 14% of the time, Pallas kernels for 0%

commit v1 on v0

--- a/solution.py
+++ b/solution.py
@@ -89,8 +89,12 @@
     )
     state = start_state
     first_row = jnp.int32(0)
-    key_part = lax.all_gather(key_in, "ctx", axis=1, tiled=True)
-    value_part = lax.all_gather(value_in, "ctx", axis=1, tiled=True)
+    _try_all_sides = lambda obj, inp, net_axis: jnp.split(
+        lax.all_gather(jnp.concatenate([obj, inp], 0), axis_name=net_axis, axis=1, tiled=True),
+        [obj.shape[0]],
+        0,
+    )
+    key_part, value_part = _try_all_sides(key_in, value_in, "ctx")
     piece_rows = key_part.shape[1]
     block_len = math.gcd(piece_rows, 512)
     for block_start in range(0, piece_rows, block_len):

time: 233 us -> 216 us (0.927)
  waiting for transfers between devices: 115 us -> 105 us
  local copies, waits for them, and re-layouts: 18.4 us -> 10.4 us
    all_gather x2 -> x1, waiting for transfers between devices: 49.4 us -> 37.1 us  [shards(): lax.all_gather(jnp.concatenate([obj, inp], 0), axis_name=net_axis, axis=1...]
    another operation x32, local copies, waits for them, and re-layouts: 9.55 us -> 0.52 us  [shards(): kernel_term = jnp.stack(kernel_rows) * factor]
    unnamed x8 -> x7, waiting for transfers between devices: 13.6 us -> 18.4 us
    all_gather x2 -> x0, local copies, waits for them, and re-layouts: 2.98 us -> none  [the longest x1 1.49 us: shards(): key_part = lax.all_gather(key_in, 'ctx', axis=1, tiled=True)]
    all_gather x1, waiting for transfers between devices: 40.7 us -> 37.8 us  [shards(): lax.all_gather(out_weight, 'fsdp', axis=1, tiled=True)]
    split x0 -> x3, local copies, waits for them, and re-layouts: none -> 2.8 us  [shards(): jnp.split(lax.all_gather(jnp.concatenate([obj, inp], 0), axis_name=net_ax...]
    unnamed x23 -> x47, local copies, waits for them, and re-layouts: 5.28 us -> 5.33 us
  transfers between devices with their start and end apart: 10 -> 9, of which waited for: 5 -> 5; matrix products, arithmetic and copies ran while one was open for 14% -> 11% of each run, Pallas kernels for 0% -> 0%
where the time goes in v1:
time: 216 us
  waiting for transfers between devices  105 us (49%)
  blocking collectives  46.3 us (21%)
  other arithmetic  21.2 us (10%)
  between operations  15.2 us (7%)
  starting transfers between devices  12.1 us (6%)
  local copies, waits for them, and re-layouts  10.4 us (5%)
  matrix products  5.75 us (3%)
    all_gather x1, waiting for transfers between devices, shards(): lax.all_gather(out_weight, 'fsdp', axis=1, tiled=True)  37.8 us
    all_gather x1, waiting for transfers between devices, shards(): lax.all_gather(jnp.concatenate([obj, inp], 0), axis_name=net_axis, axis=1...  37.1 us
    psum x1, blocking collectives, shards(): totals = lax.psum((shares[0], shares[1], shares[2]), ('ctx', 'dp'))  31 us
    unnamed x7, waiting for transfers between devices  18.4 us
    reduce_scatter x1, waiting for transfers between devices, shards(): lax.psum_scatter(kernel_term.astype(jnp.bfloat16), 'fsdp', scatter_dimens...  11.6 us
    ppermute x2, starting transfers between devices, extended(): lax.ppermute(lax.slice_in_dim(block, block.shape[dim] - width, None, axis...  9.1 us
    reduce_sum x2, other arithmetic, shards(): jnp.sum(grad_pre * conv_in[tap_index:tap_index + row_count], axis=0)  7.78 us
    all_gather x1, blocking collectives, shards(): lax.all_gather(conv_kernel, 'fsdp', axis=1, tiled=True)  6.66 us
  transfers between devices with their start and end apart: 9, of which 5 were waited for; matrix products, arithmetic and copies ran while one was open for 11% of the time, Pallas kernels for 0%

profile of v1, /device:TPU:0, one launch (start us, length us, event | category | flops | bytes accessed | tf_op | source)
XLA Modules:
  0.0 215.8 jit_solution(8472566573849929541)
XLA Ops:
  7.2 1.9 pad_maximum_fusion
  10.6 1.1 copy.24
  11.7 6.7 %all_gather.18 = f32[31,1536]{1,0:T(8,128)S(1)} all-gather(f32[31,768]{1,0:T(8,128)} %param.16), channel_id=1, replica_groups=mesh['groups'=2,'ctx'=4,'fsdp'=2,'dp'=2] {'fsdp'}, dimensions={1}, use_global_device_ids=true | all-gather | bytes 285696 | tf_op jit(solution)/shard_map/all_gather | solution.py:119
  21.1 37.1 %all-gather.5.cloned.1.call-done = bf16[2,512,1024]{2,1,0:T(8,128)(2,1)} async-done(((bf16[2,128,1024]{2,1,0:T(8,128)(2,1)}), bf16[2,512,1024]{2,1,0:T(8,128)(2,1)}) %all-gather.5.cloned.1.call-update) | async-done | bytes 2097168 | tf_op jit(solution)/shard_map/all_gather | solution.py:93
  58.2 1.7 fusion.66
  61.1 1.8 bitcast_reduce_fusion
  62.9 1.1 fusion.2
  64.1 1.5 fusion.20
  65.7 37.8 %all-gather.7.cloned.1.call-done = bf16[1024,1536]{1,0:T(8,128)(2,1)} async-done(((bf16[1024,768]{1,0:T(8,128)(2,1)}), bf16[1024,1536]{1,0:T(8,128)(2,1)}) %all-gather.7.cloned.1.call-update) | async-done | bytes 3145744 | tf_op jit(solution)/shard_map/all_gather | solution.py:114
  103.5 2.5 %fusion.4 = bf16[128,1536]{1,0:T(8,128)(2,1)S(1)} fusion(bf16[128,1024]{0,1:T(8,128)(2,1)S(1)} %bitcast.62, bf16[1024,1536]{1,0:T(8,128)(2,1)} %all-gather.7.cloned.1.call-done, bf16[1,128,1536]{2,1,0:T(8,128)(2,1)S(1)} %copy-done.1), kind=kOutput, calls=%fused_computation.8 | convolution fusion | flops 403243008 | bytes 4194304 | tf_op jit(solution)/shard_map/dot_general | solution.py:112
  106.0 1.3 collective-permute-start.1
  107.3 4.5 %collective-permute-start = (bf16[15,1536]{1,0:T(8,128)(2,1)S(1)}, bf16[15,1536]{1,0:T(8,128)(2,1)S(1)}, u32[]{:S(2)}, u32[]{:S(2)}) collective-permute-start(bf16[15,1536]{1,0:T(8,128)(2,1)S(1)} %get-tuple-element.84), channel_id=1, source_target_pairs={{0,4},{4,8},{8,12},{1,5},{5,9},{9,13},{2,6},{6,10},{10,14},{3,7},{... | collective-permute-start | bytes 138248 | tf_op jit(solution)/shard_map/ppermute | solution.py:17
  111.9 4.3 %all-gather.1 = f32[2,1,768]{2,1,0:T(1,128)S(1)} all-gather(f32[1,1,768]{2,1,0:T(1,128)S(1)} %reshape.114), channel_id=1, replica_groups=mesh['groups'=2,'ctx'=4,'fsdp'=2,'dp'=2] {'fsdp'}, dimensions={0}, use_global_device_ids=true | all-gather | bytes 9216 | tf_op jit(solution)/shard_map/all_gather | solution.py:121
  116.3 4.3 %all-gather = f32[2,1,768]{2,1,0:T(1,128)S(1)} all-gather(f32[1,1,768]{2,1,0:T(1,128)S(1)} %reshape.112), channel_id=1, replica_groups=mesh['groups'=2,'ctx'=4,'fsdp'=2,'dp'=2] {'fsdp'}, dimensions={0}, use_global_device_ids=true | all-gather | bytes 9216 | tf_op jit(solution)/shard_map/all_gather | solution.py:120
  121.8 6.3 %multiply_reduce_fusion.1 = (f32[1536]{0:T(1024)S(1)}, f32[1536]{0:T(1024)S(1)}, f32[1536]{0:T(1024)S(1)}, f32[1536]{0:T(1024)S(1)}, f32[1536]{0:T(1024)S(1)}, /...) fusion(f32[158,1536]{1,0:T(8,128)S(1)} %get-tuple-element.81, ...), kind=kLoop, calls=%fused_computation.90 | loop fusion | flops 21206016 | bytes 26653184 | tf_op jit(solution)/shard_map/reduce_sum | solution.py:146
  129.1 1.5 multiply_reduce_fusion.19
  130.6 1.3 collective-permute-start.3
  131.9 4.5 %collective-permute-start.2 = (bf16[15,1536]{1,0:T(8,128)(2,1)S(1)}, bf16[15,1536]{1,0:T(8,128)(2,1)S(1)}, u32[]{:S(2)}, u32[]{:S(2)}) collective-permute-start(bf16[15,1536]{1,0:T(8,128)(2,1)S(1)} %get-tuple-element.82), channel_id=1, source_target_pairs={{0,4},{4,8},{8,12},{1,5},{5,9},{9,13},{2,6},{6,10},{10,14},{3,7},{... | collective-permute-start | bytes 138248 | tf_op jit(solution)/shard_map/ppermute | solution.py:17
  138.6 5.4 %multiply_reduce_fusion = (f32[1536]{0:T(1024)S(1)}, f32[128]{0:T(128)S(1)}, f32[128]{0:T(128)S(1)}, f32[128,1536]{1,0:T(8,128)S(1)}) fusion(f32[158,1536]{1,0:T(8,128)S(1)} %get-tuple-element.80, f32[1536]{0:T(1024)S(1)} %reshape.115, f32[158,1536]{1,0:T(8,128)S(1)} %maximum_convert_fusion, f32[1536]{0:T(1024)S(1)} %get-tuple-element.41, ...), kind=kLoop, calls=%fused_computation.89 | loop fusion | flops 13367552 | bytes 26156544 | tf_op jit(solution)/shard_map/reduce_sum | solution.py:157
  145.9 4.4 %reduce-scatter.10.cloned.1.call-done = bf16[768,1]{1,0:T(8,128)(2,1)} async-done(((bf16[1536,1]{1,0:T(8,128)(2,1)}), bf16[768,1]{1,0:T(8,128)(2,1)}) %reduce-scatter.10.cloned.1.call-update) | async-done | bytes 1552
  151.3 1.1 fusion.58
  152.4 13.2 %reduce-scatter.12.cloned.1.call-done = bf16[768,1]{1,0:T(8,128)(2,1)} async-done(((bf16[1536,1]{1,0:T(8,128)(2,1)}), bf16[768,1]{1,0:T(8,128)(2,1)}) %reduce-scatter.12.cloned.1.call-update) | async-done | bytes 1552
  166.7 11.6 %reduce-scatter.8.cloned.1.call-done = bf16[31,768]{1,0:T(8,128)(2,1)} async-done(((bf16[31,1536]{1,0:T(8,128)(2,1)}), bf16[31,768]{1,0:T(8,128)(2,1)}) %reduce-scatter.8.cloned.1.call-update) | async-done | bytes 47632 | tf_op jit(solution)/shard_map/reduce_scatter | solution.py:159
  178.3 31.0 %all-reduce.2 = (f32[31,768]{1,0:T(8,128)}, f32[768]{0:T(1024)}, f32[768]{0:T(1024)}) all-reduce(bf16[31,768]{1,0:T(8,128)(2,1)} %reduce-scatter.8.cloned.1.call-done, f32[768]{0:T(1024)S(1)} %get-tuple-element.93, f32[768]{0:T(1024)S(1)} %get-tuple-element.92), channel_id=1, replica_groups=mesh['groups'=2,'ctx'=4,'fsdp'=2,'dp'=2] {'ctx','dp'}, use_global_device_ids=true, to_apply=%region_38.39 | all-reduce | flops 25344 | bytes 155136 | tf_op jit(solution)/shard_map/psum | solution.py:169
  (118 shorter events, 12.7 us)
Async XLA Ops:
  7.2 51.1 %all-gather.5.cloned.1.call-start = ((), (), s32[]{:S(2)}) async-start(), calls=%async_computation.3 | async-start | bytes 2621440 | tf_op jit(solution)/shard_map/all_gather | solution.py:93
  9.1 94.3 %all-gather.7.cloned.1.call-start = ((), (), s32[]{:S(2)}) async-start(), calls=%async_computation.4 | async-start | bytes 4718592 | tf_op jit(solution)/shard_map/all_gather | solution.py:114
  9.9 140.4 %reduce-scatter.10.cloned.1.call-start = ((), (), s32[]{:S(2)}) async-start(), calls=%async_computation.6 | async-start | bytes 589824
  65.5 55.7 %copy-start.16 = (f32[158]{0:T(256)S(1)}, f32[158]{0:T(256)}, u32[]{:S(2)}) copy-start(f32[158]{0:T(256)} %and_convert_fusion) | copy-start | bytes 1900
  65.6 56.1 %copy-start = (bf16[1,128,1536]{2,1,0:T(8,128)(2,1)S(1)}, bf16[1,128,1536]{2,1,0:T(8,128)(2,1)}, u32[]{:S(2)}) copy-start(bf16[1,128,1536]{2,1,0:T(8,128)(2,1)} %param.19) | copy-start | bytes 1179652
  65.6 56.1 %copy-start.2 = (f32[1536]{0:T(1024)S(1)}, f32[1536]{0:T(1024)}, u32[]{:S(2)}) copy-start(f32[1536]{0:T(1024)} %get-tuple-element.58) | copy-start | bytes 18436
  65.6 56.1 %copy-start.3 = (f32[1536]{0:T(1024)S(1)}, f32[1536]{0:T(1024)}, u32[]{:S(2)}) copy-start(f32[1536]{0:T(1024)} %get-tuple-element.59) | copy-start | bytes 18436
  65.6 56.1 %copy-start.4 = (f32[1536]{0:T(1024)S(1)}, f32[1536]{0:T(1024)}, u32[]{:S(2)}) copy-start(f32[1536]{0:T(1024)} %get-tuple-element.60) | copy-start | bytes 18436
  65.6 56.1 %copy-start.5 = (f32[1536]{0:T(1024)S(1)}, f32[1536]{0:T(1024)}, u32[]{:S(2)}) copy-start(f32[1536]{0:T(1024)} %get-tuple-element.61) | copy-start | bytes 18436
  65.6 56.1 %copy-start.6 = (f32[1536]{0:T(1024)S(1)}, f32[1536]{0:T(1024)}, u32[]{:S(2)}) copy-start(f32[1536]{0:T(1024)} %get-tuple-element.62) | copy-start | bytes 18436
  65.6 56.1 %copy-start.7 = (f32[1536]{0:T(1024)S(1)}, f32[1536]{0:T(1024)}, u32[]{:S(2)}) copy-start(f32[1536]{0:T(1024)} %get-tuple-element.63) | copy-start | bytes 18436
  65.6 56.1 %copy-start.8 = (f32[1536]{0:T(1024)S(1)}, f32[1536]{0:T(1024)}, u32[]{:S(2)}) copy-start(f32[1536]{0:T(1024)} %get-tuple-element.64) | copy-start | bytes 18436
  65.6 56.1 %copy-start.9 = (f32[1536]{0:T(1024)S(1)}, f32[1536]{0:T(1024)}, u32[]{:S(2)}) copy-start(f32[1536]{0:T(1024)} %get-tuple-element.65) | copy-start | bytes 18436
  65.6 56.1 %copy-start.10 = (f32[1536]{0:T(1024)S(1)}, f32[1536]{0:T(1024)}, u32[]{:S(2)}) copy-start(f32[1536]{0:T(1024)} %get-tuple-element.66) | copy-start | bytes 18436
  65.7 56.1 %copy-start.11 = (f32[1536]{0:T(1024)S(1)}, f32[1536]{0:T(1024)}, u32[]{:S(2)}) copy-start(f32[1536]{0:T(1024)} %get-tuple-element.67) | copy-start | bytes 18436
  65.7 56.1 %copy-start.12 = (f32[1536]{0:T(1024)S(1)}, f32[1536]{0:T(1024)}, u32[]{:S(2)}) copy-start(f32[1536]{0:T(1024)} %get-tuple-element.68) | copy-start | bytes 18436
  65.7 56.1 %copy-start.13 = (f32[1536]{0:T(1024)S(1)}, f32[1536]{0:T(1024)}, u32[]{:S(2)}) copy-start(f32[1536]{0:T(1024)} %get-tuple-element.69) | copy-start | bytes 18436
  65.7 56.1 %copy-start.14 = (f32[1536]{0:T(1024)S(1)}, f32[1536]{0:T(1024)}, u32[]{:S(2)}) copy-start(f32[1536]{0:T(1024)} %get-tuple-element.70) | copy-start | bytes 18436
  106.0 14.7 %collective-permute-start.1 = (bf16[15,1536]{1,0:T(8,128)(2,1)S(1)}, bf16[15,1536]{1,0:T(8,128)(2,1)S(1)}, u32[]{:S(2)}, u32[]{:S(2)}) collective-permute-start(bf16[15,1536]{1,0:T(8,128)(2,1)S(1)} %get-tuple-element.85), channel_id=1, source_target_pairs={{4,0},{8,4},{12,8},{5,1},{9,5},{13,9},{6,2},{10,6},{14,10},{7,3},{... | collective-permute-start | bytes 138248 | tf_op jit(solution)/shard_map/ppermute | solution.py:20
  107.3 13.4 %collective-permute-start = (bf16[15,1536]{1,0:T(8,128)(2,1)S(1)}, bf16[15,1536]{1,0:T(8,128)(2,1)S(1)}, u32[]{:S(2)}, u32[]{:S(2)}) collective-permute-start(bf16[15,1536]{1,0:T(8,128)(2,1)S(1)} %get-tuple-element.84), channel_id=1, source_target_pairs={{0,4},{4,8},{8,12},{1,5},{5,9},{9,13},{2,6},{6,10},{10,14},{3,7},{... | collective-permute-start | bytes 138248 | tf_op jit(solution)/shard_map/ppermute | solution.py:17
  130.6 7.9 %collective-permute-start.3 = (bf16[15,1536]{1,0:T(8,128)(2,1)S(1)}, bf16[15,1536]{1,0:T(8,128)(2,1)S(1)}, u32[]{:S(2)}, u32[]{:S(2)}) collective-permute-start(bf16[15,1536]{1,0:T(8,128)(2,1)S(1)} %get-tuple-element.83), channel_id=1, source_target_pairs={{4,0},{8,4},{12,8},{5,1},{9,5},{13,9},{6,2},{10,6},{14,10},{7,3},{... | collective-permute-start | bytes 138248 | tf_op jit(solution)/shard_map/ppermute | solution.py:20
  131.9 6.6 %collective-permute-start.2 = (bf16[15,1536]{1,0:T(8,128)(2,1)S(1)}, bf16[15,1536]{1,0:T(8,128)(2,1)S(1)}, u32[]{:S(2)}, u32[]{:S(2)}) collective-permute-start(bf16[15,1536]{1,0:T(8,128)(2,1)S(1)} %get-tuple-element.82), channel_id=1, source_target_pairs={{0,4},{4,8},{8,12},{1,5},{5,9},{9,13},{2,6},{6,10},{10,14},{3,7},{... | collective-permute-start | bytes 138248 | tf_op jit(solution)/shard_map/ppermute | solution.py:17
  137.9 27.7 %reduce-scatter.12.cloned.1.call-start = ((), (), s32[]{:S(2)}) async-start(), calls=%async_computation.7 | async-start | bytes 589824
  145.1 33.2 %reduce-scatter.8.cloned.1.call-start = ((), (), s32[]{:S(2)}) async-start(), calls=%async_computation.5 | async-start | bytes 147456 | tf_op jit(solution)/shard_map/reduce_scatter | solution.py:159
  (4 other events, 138.3 us)
Sparse Core Ops, SparseCore 0:
  9.6 48.6 all-gather.4
  59.8 43.6 all-gather.6
  138.1 12.1 reduce-scatter.9
  152.5 13.1 reduce-scatter.11
  168.2 9.9 reduce-scatter.7
